TPU v7x, 32 devices: a whole 2x2x4 slice. The times are simulated.
32 devices in a mesh: rep: 8 (over z, core), mdl: 4 (over y, x).
Axes of the slice: x: 2, y: 2, z: 4, core: 2. Of those that a mesh axis runs over, the one named last changes fastest.
Arguments:
- deltas: bfloat16 [8, 2560, 2560], P('rep', 'mdl'), may hold values from -72 to 72
- errors: bfloat16 [8, 2560, 2560], P('rep', 'mdl'), may hold values from -3 to 3
- starts: float32 [2560, 64], replicated, may hold values from -6 to 6
- momentum: float32 [2560, 2560], P('mdl', 'rep'), may hold values from -2 to 2
Outputs:
- new_errors: bfloat16 [8, 2560, 2560], P('rep', 'mdl')
- new_momentum: float32 [2560, 2560], P('mdl', 'rep')
- outer_step: float32 [2560, 2560], P('mdl', 'rep')
All inputs are finite; a program needn't handle non-finite values.
Results may differ from a plain program's by a relative error of at most 0.001.
Values sent between devices are 32-bit elements; how exact they have to be, the bound alone decides.
A program may use at most 64 MiB of HBM per device.

v0:
```python
import jax
import jax.numpy as jnp
from jax import lax
from jax.sharding import PartitionSpec as P

highest = lax.Precision.HIGHEST


def body(deltas, errors, starts, momentum):
    replicas = lax.axis_size("rep")
    merged = deltas[0].astype(jnp.float32) + errors[0].astype(jnp.float32)
    left_part = jnp.einsum("ac,ck->ka", merged, starts, precision=highest)
    left = lax.psum(left_part, "rep") / replicas
    gram = jnp.einsum("ka,la->kl", left, left, precision=highest)
    gram = lax.psum(gram, "mdl")
    lower = jnp.linalg.cholesky(gram)
    basis = jax.scipy.linalg.solve_triangular(lower, left, lower=True)
    right_part = jnp.einsum("ac,ka->kc", merged, basis, precision=highest)
    column_shares = lax.psum_scatter(right_part, "mdl", scatter_dimension=1, tiled=True)
    column_shares = lax.psum(column_shares, "rep")
    right = lax.all_gather(column_shares, "mdl", axis=1, tiled=True) / replicas
    approx = jnp.einsum("ka,kc->ac", basis, right, precision=highest)
    new_errors = (merged - approx).astype(jnp.bfloat16)[None]
    width = momentum.shape[1]
    owned = lax.dynamic_slice_in_dim(approx, lax.axis_index("rep") * width, width, 1)
    new_momentum = 0.9 * momentum + owned
    outer_step = 0.7 * (owned + 0.9 * new_momentum)
    return (new_errors, new_momentum, outer_step)


def solution(mesh):
    placed = (P("rep", "mdl", None), P("rep", "mdl", None), P(), P("mdl", "rep"))
    return jax.shard_map(
        body,
        mesh=mesh,
        in_specs=placed,
        out_specs=(P("rep", "mdl", None), P("mdl", "rep"), P("mdl", "rep")),
        check_vma=False,
    )
```

profile of v0, /device:TPU:0, one launch (start us, length us, event | category | flops | bytes accessed | tf_op | source)
XLA Modules:
  0.0 226.7 jit_solution(16170956885530419653)
XLA Ops:
  7.2 0.0 copy-start
  7.2 0.0 copy-start.3
  7.2 0.0 all-reduce.3.cloned.1.call-start
  7.2 1.0 copy-done
  8.3 9.4 %fusion.6 = f32[64,640]{1,0:T(8,128)} fusion(f32[2560,64]{0,1:T(8,128)S(1)} %copy-done, bf16[1,640,2560]{2,1,0:T(8,128)(2,1)} %param.5, bf16[1,640,2560]{2,1,0:T(8,128)(2,1)} %param.4), kind=kOutput, calls=%fused_computation.8 | convolution fusion | flops 1263206400 | bytes 7372800 | tf_op jit(solution)/shard_map/ac,ck->ka/dot_general | solution.py:12
  17.6 0.0 all-reduce.3.cloned.1.call-update
  17.7 0.0 reduce-scatter.2.cloned.1.call-start
  17.7 55.5 %all-reduce.3.cloned.1.call-done = f32[64,640]{1,0:T(8,128)} async-done(((f32[64,640]{1,0:T(8,128)}), f32[64,640]{1,0:T(8,128)}) %all-reduce.3.cloned.1.call-update) | async-done | bytes 163856 | tf_op jit(solution)/shard_map/psum | solution.py:13
  73.2 1.3 fusion.14
  74.5 16.2 %psum.22 = f32[64,64]{0,1:T(8,128)S(1)} all-reduce(f32[64,64]{0,1:T(8,128)S(1)} %fusion.14), channel_id=1, replica_groups=mesh['rep'=8,'mdl'=4] {'mdl'}, use_global_device_ids=true, to_apply=%region_1.0 | all-reduce | flops 4096 | bytes 32768 | tf_op jit(solution)/shard_map/psum | solution.py:15
  90.7 0.1 copy.8
  90.8 5.8 %cholesky.16 = f32[64,64]{1,0:T(8,128)S(1)} custom-call(f32[64,64]{1,0:T(8,128)S(1)} %fusion.20), custom_call_target="Cholesky" | custom-call | tf_op jit(solution)/shard_map/jit(cholesky)/cholesky | solution.py:16
  96.7 0.6 compare_reduce_fusion
  97.3 0.7 fusion.18
  98.0 4.9 %custom-call.7 = f32[1,64,64]{1,2,0:T(8,128)S(1)} custom-call(f32[1,64,64]{2,1,0:T(8,128)S(1)} %fusion.18), custom_call_target="InvertDiagBlocksLowerTriangular" | custom-call | tf_op jit(solution)/shard_map/jit(_solve_triangular)/triangular_solve | solution.py:17
  102.9 1.3 fusion.12
  104.2 8.3 %fusion = f32[64,2560]{1,0:T(8,128)} fusion(f32[64,640]{1,0:T(8,128)S(1)} %fusion.12, bf16[1,640,2560]{2,1,0:T(8,128)(2,1)} %param.5, bf16[1,640,2560]{2,1,0:T(8,128)(2,1)} %param.4), kind=kOutput, calls=%fused_computation.1 | convolution fusion | flops 1263206400 | bytes 7372800 | tf_op jit(solution)/shard_map/ac,ka->kc/dot_general | solution.py:18
  112.5 0.0 reduce-scatter.2.cloned.1.call-update
  112.5 0.0 all-reduce.5.cloned.1.call-start
  112.6 25.6 %reduce-scatter.2.cloned.1.call-done = f32[64,640]{1,0:T(8,128)} async-done(((f32[64,2560]{1,0:T(8,128)}), f32[64,640]{1,0:T(8,128)}) %reduce-scatter.2.cloned.1.call-update) | async-done | bytes 163856 | tf_op jit(solution)/shard_map/reduce_scatter | solution.py:19
  138.2 0.0 all-reduce.5.cloned.1.call-update
  138.3 0.0 copy-done.3
  138.3 0.3 copy.9
  138.6 54.7 %all-reduce.5.cloned.1.call-done = f32[64,640]{1,0:T(8,128)} async-done(((f32[64,640]{1,0:T(8,128)}), f32[64,640]{1,0:T(8,128)}) %all-reduce.5.cloned.1.call-update) | async-done | bytes 163856 | tf_op jit(solution)/shard_map/psum | solution.py:20
  193.3 0.0 copy-start.1
  193.3 0.0 copy-start.2
  193.3 13.2 %all_gather.3 = f32[64,2560]{1,0:T(8,128)S(1)} all-gather(f32[64,640]{1,0:T(8,128)} %all-reduce.5.cloned.1.call-done), channel_id=1, replica_groups=mesh['rep'=8,'mdl'=4] {'mdl'}, dimensions={1}, use_global_device_ids=true | all-gather | bytes 819200 | tf_op jit(solution)/shard_map/all_gather | solution.py:21
  206.4 5.4 %fusion.9 = f32[640,2560]{1,0:T(8,128)S(1)} fusion(f32[64,640]{1,0:T(8,128)S(1)} %fusion.12, f32[64,2560]{1,0:T(8,128)S(1)} %all_gather.3), kind=kOutput, calls=%fused_computation.11 | convolution fusion | flops 1258455040 | bytes 7372800 | tf_op jit(solution)/shard_map/ka,kc->ac/dot_general | solution.py:22
  211.9 0.0 copy-done.1
  211.9 0.0 copy-done.2
  211.9 3.3 %fusion.5 = bf16[1,640,2560]{2,1,0:T(8,128)(2,1)} fusion(f32[640,2560]{1,0:T(8,128)S(1)} %fusion.9, bf16[1,640,2560]{2,1,0:T(8,128)(2,1)S(1)} %copy-done.1, bf16[1,640,2560]{2,1,0:T(8,128)(2,1)S(1)} %copy-done.2), kind=kLoop, calls=%fused_computation.7 | loop fusion | flops 8192000 | bytes 16384000 | tf_op jit(solution)/shard_map/broadcast_in_dim | solution.py:23
  215.2 1.3 add_multiply_fusion
  216.5 2.4 %copy.10 = f32[640,320]{0,1:T(8,128)} copy(f32[640,320]{1,0:T(8,128)} %get-tuple-element.7) | data formatting | bytes 1638400
  218.9 1.2 copy.11
  (2 shorter events, 0.0 us)
Async XLA Ops:
  7.2 1.1 copy-start
  7.2 131.1 %copy-start.3 = (f32[640,320]{0,1:T(8,128)S(1)}, f32[640,320]{0,1:T(8,128)}, u32[]{:S(2)}) copy-start(f32[640,320]{0,1:T(8,128)} %param.7) | copy-start | bytes 2457604
  7.2 66.0 %all-reduce.3.cloned.1.call-start = ((), (), s32[]{:S(2)}) async-start(), calls=%async_computation.1 | async-start | bytes 327680 | tf_op jit(solution)/shard_map/psum | solution.py:13
  17.7 120.6 %reduce-scatter.2.cloned.1.call-start = ((), (), s32[]{:S(2)}) async-start(), calls=%async_computation.2 | async-start | bytes 819200 | tf_op jit(solution)/shard_map/reduce_scatter | solution.py:19
  112.5 80.7 %all-reduce.5.cloned.1.call-start = ((), (), s32[]{:S(2)}) async-start(), calls=%async_computation.3 | async-start | bytes 327680 | tf_op jit(solution)/shard_map/psum | solution.py:20
  193.3 18.6 %copy-start.1 = (bf16[1,640,2560]{2,1,0:T(8,128)(2,1)S(1)}, bf16[1,640,2560]{2,1,0:T(8,128)(2,1)}, u32[]{:S(2)}) copy-start(bf16[1,640,2560]{2,1,0:T(8,128)(2,1)} %param.5) | copy-start | bytes 9830404
  193.3 18.6 %copy-start.2 = (bf16[1,640,2560]{2,1,0:T(8,128)(2,1)S(1)}, bf16[1,640,2560]{2,1,0:T(8,128)(2,1)}, u32[]{:S(2)}) copy-start(bf16[1,640,2560]{2,1,0:T(8,128)(2,1)} %param.4) | copy-start | bytes 9830404
Sparse Core Ops, SparseCore 0:
  17.8 55.3 all-reduce.2
  112.7 25.5 reduce-scatter.1
  140.6 52.6 all-reduce.4
where the time goes:
time: 227 us
  waiting for transfers between devices  136 us (60%)
  blocking collectives  29.4 us (13%)
  matrix products  25.7 us (11%)
  other arithmetic  16.7 us (7%)
  between operations  13.8 us (6%)
  local copies, waits for them, and re-layouts  5.06 us (2%)
    psum x1, waiting for transfers between devices, body(): left = lax.psum(left_part, 'rep') / replicas  55.5 us
    psum x1, waiting for transfers between devices, body(): column_shares = lax.psum(column_shares, 'rep')  54.7 us
    reduce_scatter x1, waiting for transfers between devices, body(): lax.psum_scatter(right_part, 'mdl', scatter_dimension=1, tiled=True)  25.6 us
    psum x1, blocking collectives, body(): gram = lax.psum(gram, 'mdl')  16.2 us
    all_gather x1, blocking collectives, body(): right = lax.all_gather(column_shares, 'mdl', axis=1, tiled=True) / replicas  13.2 us
    dot_general x1, matrix products, body(): left_part = jnp.einsum('ac,ck->ka', merged, starts, precision=highest)  9.37 us
    dot_general x1, matrix products, body(): right_part = jnp.einsum('ac,ka->kc', merged, basis, precision=highest)  8.35 us
    another operation x3, other arithmetic, body(): lower = jnp.linalg.cholesky(gram)  6.52 us
  transfers between devices with their start and end apart: 3, of which 3 were waited for; matrix products, arithmetic and copies ran while one was open for 0% of the time, Pallas kernels for 0%

commit v1 on v0

--- a/solution.py
+++ b/solution.py
@@ -17,7 +17,11 @@
     basis = jax.scipy.linalg.solve_triangular(lower, left, lower=True)
     right_part = jnp.einsum("ac,ka->kc", merged, basis, precision=highest)
     column_shares = lax.psum_scatter(right_part, "mdl", scatter_dimension=1, tiled=True)
-    column_shares = lax.psum(column_shares, "rep")
+    column_shares = column_shares
+    for hop in (1, 2, 4):
+        column_shares = column_shares + lax.ppermute(
+            column_shares, "rep", [(dev, dev ^ hop) for dev in range(8)]
+        )
     right = lax.all_gather(column_shares, "mdl", axis=1, tiled=True) / replicas
     approx = jnp.einsum("ka,kc->ac", basis, right, precision=highest)
     new_errors = (merged - approx).astype(jnp.bfloat16)[None]

time: 227 us -> 190 us (0.84)
  waiting for transfers between devices: 136 us -> 94.6 us
  starting transfers between devices: 0.12 us -> 4.09 us
    psum x1 -> x0, waiting for transfers between devices: 54.7 us -> none  [body(): column_shares = lax.psum(column_shares, 'rep')]
    ppermute x0 -> x3, waiting for transfers between devices: none -> 13.4 us  [body(): lax.ppermute(column_shares, 'rep', [(dev, dev ^ hop) for dev in range(8)])]
    ppermute x0 -> x3, starting transfers between devices: none -> 4.01 us  [body(): lax.ppermute(column_shares, 'rep', [(dev, dev ^ hop) for dev in range(8)])]
  transfers between devices with their start and end apart: 3 -> 5, of which waited for: 3 -> 5; matrix products, arithmetic and copies ran while one was open for 0% -> 0% of each run, Pallas kernels for 0% -> 0%
where the time goes in v1:
time: 190 us; the launch traced here: 189 us
  waiting for transfers between devices  94.6 us (50%)
  blocking collectives  28.1 us (15%)
  matrix products  25.7 us (14%)
  other arithmetic  17.7 us (9%)
  between operations  14.1 us (7%)
  local copies, waits for them, and re-layouts  5.08 us (3%)
  starting transfers between devices  4.09 us (2%)
    psum x1, waiting for transfers between devices, body(): left = lax.psum(left_part, 'rep') / replicas  55.5 us
    reduce_scatter x1, waiting for transfers between devices, body(): lax.psum_scatter(right_part, 'mdl', scatter_dimension=1, tiled=True)  25.7 us
    psum x1, blocking collectives, body(): gram = lax.psum(gram, 'mdl')  16.2 us
    ppermute x3, waiting for transfers between devices, body(): lax.ppermute(column_shares, 'rep', [(dev, dev ^ hop) for dev in range(8)])  13.4 us
    all_gather x1, blocking collectives, body(): right = lax.all_gather(column_shares, 'mdl', axis=1, tiled=True) / replicas  11.9 us
    dot_general x1, matrix products, body(): left_part = jnp.einsum('ac,ck->ka', merged, starts, precision=highest)  9.38 us
    dot_general x1, matrix products, body(): right_part = jnp.einsum('ac,ka->kc', merged, basis, precision=highest)  8.35 us
    another operation x3, other arithmetic, body(): lower = jnp.linalg.cholesky(gram)  6.52 us
  transfers between devices with their start and end apart: 5, of which 5 were waited for; matrix products, arithmetic and copies ran while one was open for 0% of the time, Pallas kernels for 0%

profile of v1, /device:TPU:0, one launch (start us, length us, event | category | flops | bytes accessed | tf_op | source)
XLA Modules:
  0.0 189.4 jit_solution(16816747590317281007)
XLA Ops:
  7.2 0.0 copy-start
  7.2 0.0 all-reduce.2.cloned.1.call-start
  7.2 1.0 copy-done
  8.3 9.4 %fusion.6 = f32[64,640]{1,0:T(8,128)} fusion(f32[2560,64]{0,1:T(8,128)S(1)} %copy-done, bf16[1,640,2560]{2,1,0:T(8,128)(2,1)} %param.5, bf16[1,640,2560]{2,1,0:T(8,128)(2,1)} %param.4), kind=kOutput, calls=%fused_computation.8 | convolution fusion | flops 1263206400 | bytes 7372800 | tf_op jit(solution)/shard_map/ac,ck->ka/dot_general | solution.py:12
  17.6 0.0 copy-start.3
  17.6 0.0 all-reduce.2.cloned.1.call-update
  17.7 0.0 reduce-scatter.2.cloned.1.call-start
  17.7 55.5 %all-reduce.2.cloned.1.call-done = f32[64,640]{1,0:T(8,128)} async-done(((f32[64,640]{1,0:T(8,128)}), f32[64,640]{1,0:T(8,128)}) %all-reduce.2.cloned.1.call-update) | async-done | bytes 163856 | tf_op jit(solution)/shard_map/psum | solution.py:13
  73.2 1.3 fusion.14
  74.5 16.2 %psum.15 = f32[64,64]{0,1:T(8,128)S(1)} all-reduce(f32[64,64]{0,1:T(8,128)S(1)} %fusion.14), channel_id=1, replica_groups=mesh['rep'=8,'mdl'=4] {'mdl'}, use_global_device_ids=true, to_apply=%region_1.0 | all-reduce | flops 4096 | bytes 32768 | tf_op jit(solution)/shard_map/psum | solution.py:15
  90.7 0.1 copy.8
  90.8 5.8 %cholesky.16 = f32[64,64]{1,0:T(8,128)S(1)} custom-call(f32[64,64]{1,0:T(8,128)S(1)} %fusion.20), custom_call_target="Cholesky" | custom-call | tf_op jit(solution)/shard_map/jit(cholesky)/cholesky | solution.py:16
  96.7 0.6 compare_reduce_fusion
  97.3 0.7 fusion.18
  98.0 4.9 %custom-call.7 = f32[1,64,64]{1,2,0:T(8,128)S(1)} custom-call(f32[1,64,64]{2,1,0:T(8,128)S(1)} %fusion.18), custom_call_target="InvertDiagBlocksLowerTriangular" | custom-call | tf_op jit(solution)/shard_map/jit(_solve_triangular)/triangular_solve | solution.py:17
  102.9 1.3 fusion.12
  104.2 8.3 %fusion = f32[64,2560]{1,0:T(8,128)} fusion(f32[64,640]{1,0:T(8,128)S(1)} %fusion.12, bf16[1,640,2560]{2,1,0:T(8,128)(2,1)} %param.5, bf16[1,640,2560]{2,1,0:T(8,128)(2,1)} %param.4), kind=kOutput, calls=%fused_computation.1 | convolution fusion | flops 1263206400 | bytes 7372800 | tf_op jit(solution)/shard_map/ac,ka->kc/dot_general | solution.py:18
  112.5 0.0 reduce-scatter.2.cloned.1.call-update
  112.6 25.7 %reduce-scatter.2.cloned.1.call-done = f32[64,640]{1,0:T(8,128)} async-done(((f32[64,2560]{1,0:T(8,128)}), f32[64,640]{1,0:T(8,128)}) %reduce-scatter.2.cloned.1.call-update) | async-done | bytes 163856 | tf_op jit(solution)/shard_map/reduce_scatter | solution.py:19
  138.2 0.0 collective-permute-start
  138.2 1.6 collective-permute-done
  139.8 0.9 add.45
  140.8 1.5 collective-permute-start.1
  142.3 4.8 %collective-permute-done.1 = f32[64,640]{1,0:T(8,128)S(1)} collective-permute-done((f32[64,640]{1,0:T(8,128)S(1)}, f32[64,640]{1,0:T(8,128)S(1)}, u32[]{:S(2)}, u32[]{:S(2)}) %collective-permute-start.1) | collective-permute-done | bytes 163872 | tf_op jit(solution)/shard_map/ppermute | solution.py:22
  147.1 2.5 %collective-permute-start.2 = (f32[64,640]{1,0:T(8,128)S(1)}, f32[64,640]{1,0:T(8,128)S(1)}, u32[]{:S(2)}, u32[]{:S(2)}) collective-permute-start(f32[64,640]{1,0:T(8,128)S(1)} %add.46), channel_id=1, source_target_pairs={{0,16},{4,20},{8,24},{12,28},{16,0},{20,4},{24,8},{28,12},{1,17},{... | collective-permute-start | bytes 491528 | tf_op jit(solution)/shard_map/ppermute | solution.py:22
  149.6 0.0 copy-done.3
  149.6 0.3 copy.9
  149.9 0.0 copy-start.1
  149.9 0.0 copy-start.2
  149.9 7.0 %collective-permute-done.2 = f32[64,640]{1,0:T(8,128)S(1)} collective-permute-done((f32[64,640]{1,0:T(8,128)S(1)}, f32[64,640]{1,0:T(8,128)S(1)}, u32[]{:S(2)}, u32[]{:S(2)}) %collective-permute-start.2) | collective-permute-done | bytes 163872 | tf_op jit(solution)/shard_map/ppermute | solution.py:22
  157.0 11.9 %all_gather.3 = f32[64,2560]{1,0:T(8,128)S(1)} all-gather(f32[64,640]{1,0:T(8,128)S(1)} %add.47), channel_id=1, replica_groups=mesh['rep'=8,'mdl'=4] {'mdl'}, dimensions={1}, use_global_device_ids=true | all-gather | bytes 819200 | tf_op jit(solution)/shard_map/all_gather | solution.py:25
  168.9 5.4 %fusion.9 = f32[640,2560]{1,0:T(8,128)S(1)} fusion(f32[64,640]{1,0:T(8,128)S(1)} %fusion.12, f32[64,2560]{1,0:T(8,128)S(1)} %all_gather.3), kind=kOutput, calls=%fused_computation.11 | convolution fusion | flops 1258455040 | bytes 7372800 | tf_op jit(solution)/shard_map/ka,kc->ac/dot_general | solution.py:26
  174.3 0.0 copy-done.1
  174.3 0.0 copy-done.2
  174.3 3.3 %fusion.5 = bf16[1,640,2560]{2,1,0:T(8,128)(2,1)} fusion(f32[640,2560]{1,0:T(8,128)S(1)} %fusion.9, bf16[1,640,2560]{2,1,0:T(8,128)(2,1)S(1)} %copy-done.1, bf16[1,640,2560]{2,1,0:T(8,128)(2,1)S(1)} %copy-done.2), kind=kLoop, calls=%fused_computation.7 | loop fusion | flops 8192000 | bytes 16384000 | tf_op jit(solution)/shard_map/broadcast_in_dim | solution.py:27
  177.7 1.3 add_multiply_fusion
  179.0 2.4 %copy.10 = f32[640,320]{0,1:T(8,128)} copy(f32[640,320]{1,0:T(8,128)} %get-tuple-element.7) | data formatting | bytes 1638400
  181.4 1.2 copy.11
  (4 shorter events, 0.1 us)
Async XLA Ops:
  7.2 1.1 copy-start
  7.2 66.0 %all-reduce.2.cloned.1.call-start = ((), (), s32[]{:S(2)}) async-start(), calls=%async_computation.1 | async-start | bytes 327680 | tf_op jit(solution)/shard_map/psum | solution.py:13
  17.6 131.9 %copy-start.3 = (f32[640,320]{0,1:T(8,128)S(1)}, f32[640,320]{0,1:T(8,128)}, u32[]{:S(2)}) copy-start(f32[640,320]{0,1:T(8,128)} %param.7) | copy-start | bytes 2457604
  17.7 120.6 %reduce-scatter.2.cloned.1.call-start = ((), (), s32[]{:S(2)}) async-start(), calls=%async_computation.2 | async-start | bytes 819200 | tf_op jit(solution)/shard_map/reduce_scatter | solution.py:19
  138.2 1.6 collective-permute-start
  140.8 6.3 %collective-permute-start.1 = (f32[64,640]{1,0:T(8,128)S(1)}, f32[64,640]{1,0:T(8,128)S(1)}, u32[]{:S(2)}, u32[]{:S(2)}) collective-permute-start(f32[64,640]{1,0:T(8,128)S(1)} %add.45), channel_id=1, source_target_pairs={{0,8},{4,12},{8,0},{12,4},{16,24},{20,28},{24,16},{28,20},{1,9},{5... | collective-permute-start | bytes 491528 | tf_op jit(solution)/shard_map/ppermute | solution.py:22
  147.1 9.9 %collective-permute-start.2 = (f32[64,640]{1,0:T(8,128)S(1)}, f32[64,640]{1,0:T(8,128)S(1)}, u32[]{:S(2)}, u32[]{:S(2)}) collective-permute-start(f32[64,640]{1,0:T(8,128)S(1)} %add.46), channel_id=1, source_target_pairs={{0,16},{4,20},{8,24},{12,28},{16,0},{20,4},{24,8},{28,12},{1,17},{... | collective-permute-start | bytes 491528 | tf_op jit(solution)/shard_map/ppermute | solution.py:22
  149.9 24.4 %copy-start.1 = (bf16[1,640,2560]{2,1,0:T(8,128)(2,1)S(1)}, bf16[1,640,2560]{2,1,0:T(8,128)(2,1)}, u32[]{:S(2)}) copy-start(bf16[1,640,2560]{2,1,0:T(8,128)(2,1)} %param.5) | copy-start | bytes 9830404
  149.9 24.4 %copy-start.2 = (bf16[1,640,2560]{2,1,0:T(8,128)(2,1)S(1)}, bf16[1,640,2560]{2,1,0:T(8,128)(2,1)}, u32[]{:S(2)}) copy-start(bf16[1,640,2560]{2,1,0:T(8,128)(2,1)} %param.4) | copy-start | bytes 9830404
Sparse Core Ops, SparseCore 0:
  17.8 55.3 all-reduce.1
  112.7 25.4 reduce-scatter.1
